TPU v7x, 32 devices: a whole 2x2x4 slice. The times are simulated.
32 devices in a mesh: groups: 2 (over y), expert: 4 (over z), rep: 4 (over x, core).
Axes of the slice: x: 2, y: 2, z: 4, core: 2. Of those that a mesh axis runs over, the one named last changes fastest.
Arguments:
- tokens: bfloat16 [128, 4096], P(('groups', 'expert', 'rep')), parts along dimension 0, may hold values from -6 to 6
- expert_ids: int32 [128, 8], P(('groups', 'expert', 'rep')), parts along dimension 0, may hold values from 0 to 31, as said below
- route_probs: float32 [128, 8], P(('groups', 'expert', 'rep')), parts along dimension 0, may hold values from 0.3 to 1
- gate_weight: bfloat16 [32, 1536, 4096], P('expert', 'rep'), may hold values from -0.09375 to 0.09375
- up_weight: bfloat16 [32, 1536, 4096], P('expert', 'rep'), may hold values from -0.09375 to 0.09375
- down_weight: bfloat16 [32, 1536, 4096], P('expert', 'rep'), may hold values from -0.15625 to 0.15625
Outputs:
- moe_out: bfloat16 [128, 4096], P(('groups', 'expert', 'rep')), parts along dimension 0
There are 2 independent parts, one for each index of `groups`. A program takes and returns all parts, laid end to end along the dimension named above; an argument that names none is the same for every part. Nothing has to cross between parts.
Inputs may be any that keep to these rules, and one draw needn't show every extreme that they name: `expert_ids`: each row names 8 different experts. Among the rows of one device no expert is named more than 3 times, and some expert is named exactly 3 times among the rows of every device.
All inputs are finite; a program needn't handle non-finite values.
Results may differ from a plain program's by a relative error of at most 0.0058.
Values may be sent and summed in bfloat16 or wider, within the bound.
A program may use at most 128 MiB of HBM per device.

v0:
```python
import functools

import jax
import jax.numpy as jnp
from jax import lax
from jax.experimental import pallas as pl
from jax.experimental.pallas import tpu as pltpu
from jax.sharding import PartitionSpec as P

MESH = pl.DeviceIdType.MESH
LANES = 128
CHUNKS = 8
DEPTH = 5
LAG = 5


def kernel(
    dims,
    tok_ref,
    ids_ref,
    probs_ref,
    gate_hbm,
    up_hbm,
    down_hbm,
    out_ref,
    blocks,
    rows_ref,
    route_ref,
    hid_ref,
    cat_ref,
    pair_buf,
    down_buf,
    part_ref,
    own_ref,
    send_a,
    recv_a,
    sum_ref,
    send_c,
    recv_c,
    gate_sem,
    up_sem,
    down_sem,
    z_send,
    z_recv,
    x_send,
    x_recv,
    c_send,
    c_recv,
    a_send_sem,
    a_recv_sem,
    s_send_sem,
    s_recv_sem,
    cols_ref,
):
    Z, R, EL, TOK, D, CW, NB = dims
    NX = R // 2
    HID = gate_hbm.shape[1]
    NC = D // CW
    z = lax.axis_index("expert")
    r = lax.axis_index("rep")
    x = r // 2
    core = lax.rem(r, 2)
    mate = x * 2 + 1 - core

    def z_peer(k):
        return lax.rem(z + k, Z)

    def r_peer(k):
        return lax.rem(r + k, R)

    def x_peer(j):
        return lax.rem(x + j, NX) * 2 + core

    def gate_copy(e):
        s = lax.rem(e, NB)
        return pltpu.make_async_copy(gate_hbm.at[e], pair_buf.at[s, pl.ds(0, HID)], gate_sem.at[s])

    def up_copy(e):
        s = lax.rem(e, NB)
        return pltpu.make_async_copy(up_hbm.at[e], pair_buf.at[s, pl.ds(HID, HID)], up_sem.at[s])

    def down_copy(c):
        return pltpu.make_async_copy(
            down_hbm.at[:, :, pl.ds(pl.multiple_of(c * CW, CW), CW)], down_buf.at[c], down_sem.at[c]
        )

    def start_expert(e, carry):
        gate_copy(e).start()
        up_copy(e).start()
        return carry

    barrier = pltpu.get_barrier_semaphore()
    for k in range(1, Z):
        pl.semaphore_signal(barrier, inc=1, device_id={"expert": z_peer(k)}, device_id_type=MESH)
    for k in range(1, R):
        pl.semaphore_signal(barrier, inc=1, device_id={"rep": r_peer(k)}, device_id_type=MESH)

    lax.fori_loop(0, NB, start_expert, 0)
    EARLY = min(3, NC)
    for c in range(EARLY):
        down_copy(c).start()

    probs = probs_ref[...]
    ids = ids_ref[...]
    weights = probs / jnp.sum(probs, axis=1, keepdims=True)
    lane = lax.broadcasted_iota(jnp.int32, (TOK, LANES), 1)
    route = jnp.zeros((TOK, LANES), jnp.float32)
    for k in range(ids.shape[1]):
        route = route + jnp.where(ids[:, k : k + 1] == lane, weights[:, k : k + 1], 0.0)
    high = route.astype(jnp.bfloat16)
    low = (route - high.astype(jnp.float32)).astype(jnp.bfloat16)
    blocks[r, z, :, pl.ds(0, D)] = tok_ref[...]
    blocks[r, z, :, pl.ds(D, LANES)] = high
    blocks[r, z, :, pl.ds(D + LANES, LANES)] = low

    pl.semaphore_wait(barrier, Z - 1 + R - 1)

    def remote(src, dst, send, recv, device):
        return pltpu.make_async_remote_copy(
            src_ref=src, dst_ref=dst, send_sem=send, recv_sem=recv, device_id=device, device_id_type=MESH
        )

    def z_copy(k):
        b = blocks.at[r, z]
        return remote(b, b, z_send, z_recv.at[k - 1], {"expert": z_peer(k)})

    def x_copy(j, k):
        b = blocks.at[r, lax.rem(z + Z - k, Z)]
        return remote(b, b, x_send.at[j - 1], x_recv.at[j - 1, k], {"rep": x_peer(j)})

    def core_copy(j, k):
        b = blocks.at[lax.rem(x + NX - j, NX) * 2 + core, lax.rem(z + Z - k, Z)]
        return remote(b, b, c_send.at[j], c_recv.at[j], {"rep": mate})

    def landed(ref, sem):
        pltpu.make_async_copy(ref, ref, sem).wait()

    for k in range(1, Z):
        z_copy(k).start()
    for k in range(Z):
        if k:
            landed(blocks.at[r, lax.rem(z + Z - k, Z)], z_recv.at[k - 1])
        for j in range(1, NX):
            x_copy(j, k).start()
        core_copy(0, k).start()
    for k in range(Z):
        for j in range(1, NX):
            landed(
                blocks.at[lax.rem(x + NX - j, NX) * 2 + core, lax.rem(z + Z - k, Z)],
                x_recv.at[j - 1, k],
            )
            core_copy(j, k).start()
    for j in range(NX):
        landed(blocks.at[lax.rem(x + NX - j, NX) * 2 + 1 - core], c_recv.at[j])

    per = 16 // TOK
    groups = R * Z // per

    def gather_rows(g, carry):
        first = g * per
        rr = first // Z
        zz = lax.rem(first, Z)
        at = pl.ds(pl.multiple_of(g * 16, 16), 16)
        for piece in range(0, D, 1024):
            cols = pl.ds(piece, 1024)
            rows_ref[at, cols] = jnp.concatenate(
                [blocks[rr, zz + i, :, cols].astype(jnp.float32) for i in range(per)], axis=0
            ).astype(jnp.bfloat16)
        route_ref[at, :] = jnp.concatenate(
            [
                blocks[rr, zz + i, :, pl.ds(D, LANES)].astype(jnp.float32)
                + blocks[rr, zz + i, :, pl.ds(D + LANES, LANES)].astype(jnp.float32)
                for i in range(per)
            ],
            axis=0,
        )
        return carry

    lax.fori_loop(0, groups, gather_rows, 0)

    T = R * Z * TOK
    cols_ref[...] = rows_ref[...].T
    nt = (((1,), (1,)), ((), ()))

    def expert(e, carry):
        s = lax.rem(e, NB)
        gate_copy(e).wait()
        up_copy(e).wait()
        both = jnp.dot(pair_buf[s], cols_ref[...], preferred_element_type=jnp.float32)
        gate, up = both[:HID, :], both[HID:, :]
        spot = lax.broadcasted_iota(jnp.int32, (T, LANES), 1) == z * EL + e
        scale = jnp.sum(jnp.where(spot, route_ref[...], 0.0), axis=1, keepdims=True)
        hid_ref[e] = ((gate / (1.0 + jnp.exp(-gate)) * up).T * scale).astype(jnp.bfloat16)

        @pl.when(e + NB < EL)
        def _():
            start_expert(e + NB, 0)

        @pl.when(e + EARLY < NC)
        def _():
            down_copy(e + EARLY).start()

        return carry

    lax.fori_loop(0, EL, expert, 0)
    for c in range(EL + EARLY, NC):
        down_copy(c).start()
    cat_ref[...] = jnp.concatenate([hid_ref[e] for e in range(EL)], axis=1)

    ZT = Z * TOK

    def a_copy(c, k):
        return remote(
            send_a.at[c, r_peer(k)], recv_a.at[c, k - 1], a_send_sem.at[c], a_recv_sem.at[c], {"rep": r_peer(k)}
        )

    def s_copy(c, k):
        return remote(
            send_c.at[c, z_peer(k)], recv_c.at[c, k - 1], s_send_sem.at[c], s_recv_sem.at[c], {"expert": z_peer(k)}
        )

    def multiply(c):
        down_copy(c).wait()
        part = jnp.dot(
            cat_ref[...], down_buf[c].reshape(cat_ref.shape[1], CW), preferred_element_type=jnp.float32
        ).reshape(R, ZT, CW)
        part_ref[...] = part
        own_ref[c] = part_ref[r]
        send_a[c] = part.astype(jnp.bfloat16)
        for k in range(1, R):
            a_copy(c, k).start()

    def second(c):
        landed(recv_a.at[c], a_recv_sem.at[c])
        total = own_ref[c]
        for k in range(1, R):
            total = total + recv_a[c, k - 1].astype(jnp.float32)
        for i in range(Z):
            piece = total[i * TOK : (i + 1) * TOK, :]
            sum_ref[c, i] = piece
            send_c[c, i] = piece.astype(jnp.bfloat16)
        for k in range(1, Z):
            s_copy(c, k).start()

    def third(c):
        landed(recv_c.at[c], s_recv_sem.at[c])
        total = sum_ref[c, z]
        for k in range(1, Z):
            total = total + recv_c[c, k - 1].astype(jnp.float32)
        out_ref[:, pl.ds(pl.multiple_of(c * CW, CW), CW)] = total.astype(jnp.bfloat16)

    def step(c, carry):
        multiply(c)
        pl.when(c >= LAG)(lambda: second(c - LAG))
        return carry

    def late(c, carry):
        second(c)
        return carry

    def finish(c, carry):
        third(c)
        return carry

    lax.fori_loop(0, NC, step, 0)
    lax.fori_loop(NC - LAG, NC, late, 0)
    lax.fori_loop(0, NC, finish, 0)

    landed(blocks.at[0, pl.ds(0, Z - 1)], z_send)
    for j in range(1, NX):
        landed(blocks.at[0], x_send.at[j - 1])
    for j in range(NX):
        landed(blocks.at[0], c_send.at[j])

    def drain(c, carry):
        landed(recv_a.at[c], a_send_sem.at[c])
        landed(recv_c.at[c], s_send_sem.at[c])
        return carry

    lax.fori_loop(0, NC, drain, 0)


def solution(mesh):
    Z, R = mesh.shape["expert"], mesh.shape["rep"]

    def local(tokens, expert_ids, route_probs, gate_weight, up_weight, down_weight):
        TOK, D = tokens.shape
        EL, HID, _ = gate_weight.shape
        NB = min(DEPTH, EL)
        CW = D // CHUNKS
        T = Z * R * TOK
        NX = R // 2
        bf16, f32 = jnp.bfloat16, jnp.float32
        vmem = pl.BlockSpec(memory_space=pltpu.VMEM)
        hbm = pl.BlockSpec(memory_space=pl.ANY)
        dma = pltpu.SemaphoreType.DMA
        return pl.pallas_call(
            functools.partial(kernel, (Z, R, EL, TOK, D, CW, NB)),
            out_shape=jax.ShapeDtypeStruct((TOK, D), bf16),
            in_specs=[vmem, vmem, vmem, hbm, hbm, hbm],
            out_specs=vmem,
            scratch_shapes=[
                pltpu.VMEM((R, Z, TOK, D + 2 * LANES), bf16),
                pltpu.VMEM((T, D), bf16),
                pltpu.VMEM((T, LANES), f32),
                pltpu.VMEM((EL, T, HID), bf16),
                pltpu.VMEM((T, EL * HID), bf16),
                pltpu.VMEM((NB, 2 * HID, D), bf16),
                pltpu.VMEM((CHUNKS, EL, HID, CW), bf16),
                pltpu.VMEM((R, Z * TOK, CW), f32),
                pltpu.VMEM((CHUNKS, Z * TOK, CW), f32),
                pltpu.VMEM((CHUNKS, R, Z * TOK, CW), bf16),
                pltpu.VMEM((CHUNKS, R - 1, Z * TOK, CW), bf16),
                pltpu.VMEM((CHUNKS, Z, TOK, CW), f32),
                pltpu.VMEM((CHUNKS, Z, TOK, CW), bf16),
                pltpu.VMEM((CHUNKS, Z - 1, TOK, CW), bf16),
                dma((NB,)),
                dma((NB,)),
                dma((CHUNKS,)),
                dma,
                dma((Z - 1,)),
                dma((NX - 1,)),
                dma((NX - 1, Z)),
                dma((NX,)),
                dma((NX,)),
                dma((CHUNKS,)),
                dma((CHUNKS,)),
                dma((CHUNKS,)),
                dma((CHUNKS,)),
                pltpu.VMEM((D, T), bf16),
            ],
            compiler_params=pltpu.CompilerParams(
                collective_id=0, has_side_effects=True, vmem_limit_bytes=67_043_328
            ),
        )(tokens, expert_ids, route_probs, gate_weight, up_weight, down_weight)

    token_spec = P(("groups", "expert", "rep"), None)
    weight_spec = P("expert", "rep", None)
    return jax.shard_map(
        local,
        mesh=mesh,
        in_specs=(token_spec, token_spec, token_spec, weight_spec, weight_spec, weight_spec),
        out_specs=token_spec,
        check_vma=False,
    )
```

profile of v0, /device:TPU:0, one launch (start us, length us, event | category | flops | bytes accessed | tf_op | source)
XLA Modules:
  0.0 44.3 jit_solution(4669274849806091312)
XLA Ops:
  0.0 42.9 %shard_map.64 = bf16[4,4096]{1,0:T(4,128)(2,1)} custom-call(bf16[4,4096]{1,0:T(4,128)(2,1)} %tok_ref.1, s32[4,8]{1,0:T(4,128)} %ids_ref.1, f32[4,8]{1,0:T(4,128)} %probs_ref.1, bf16[8,384,4096]{2,1,0:T(8,128)(2,1)} %gate_hbm.1, bf16[8,384,4096]{2,1,0:T(8,128)(2,1)} %up_hbm.1, bf16[8,384,4096]{2,1,0:T(8,128)(2,1)} %down_hbm.1), custom_call_target="tpu_custom_call" | custom-call | tf_op jit(solution)/shard_map/pallas_call | solution.py:297
  42.9 1.4 %copy.8 = bf16[4,4096]{1,0:T(4,128)(2,1)} copy(bf16[4,4096]{1,0:T(4,128)(2,1)} %shard_map.64) | data formatting | bytes 65536
where the time goes:
time: 44.5 us; the launch traced here: 44.3 us
  Pallas kernels  42.9 us (96%)
  local copies, waits for them, and re-layouts  1.39 us (3%)
    pallas_call x1, Pallas kernels, local(): pl.pallas_call(functools.partial(kernel, (Z, R, EL, TOK, D, CW, NB)), out...  42.9 us
    unnamed x1, local copies, waits for them, and re-layouts  1.39 us

commit v1 on v0

--- a/solution.py
+++ b/solution.py
@@ -1,4 +1,5 @@
 import functools
+import math
 
 import jax
 import jax.numpy as jnp
@@ -12,9 +13,12 @@
 CHUNKS = 8
 DEPTH = 5
 LAG = 5
-
-
-def kernel(
+PIECES = 4
+FIRST_LAG = 3
+SHARED_BYTES = 56 << 20
+
+
+def wide_kernel(
     dims,
     tok_ref,
     ids_ref,
@@ -280,10 +284,392 @@
     lax.fori_loop(0, NC, drain, 0)
 
 
+def shared_kernel(
+    dims,
+    tok_hbm,
+    ids_hbm,
+    probs_hbm,
+    gate_hbm,
+    up_hbm,
+    down_hbm,
+    out_ref,
+    blocks,
+    route,
+    ids_ref,
+    probs_ref,
+    rows_ref,
+    weight_ref,
+    pair_buf,
+    down_buf,
+    acc_ref,
+    hid_ref,
+    cat_ref,
+    part_ref,
+    own_a,
+    send_a,
+    recv_a,
+    sum_ref,
+    own_b,
+    send_b,
+    recv_b,
+    own_c,
+    send_c,
+    recv_c,
+    tok_sem,
+    small_sem,
+    gate_sem,
+    up_sem,
+    down_sem,
+    fall_send,
+    rise_send,
+    z_recv,
+    plane_send,
+    plane_recv,
+    mate_send,
+    mate_recv,
+    a_send_sem,
+    a_recv_sem,
+    b_send_sem,
+    b_recv_sem,
+    c_send_sem,
+    c_recv_sem,
+):
+    G, Z, R, EL, HH, TOK, D, Q, CH = dims
+    NX = R // 2
+    P = NX * G
+    KC, CW = D // Q, D // CH
+    ZT = Z * TOK
+    HALF = P * ZT
+    T = 2 * HALF
+    f32, bf16 = jnp.float32, jnp.bfloat16
+    g = lax.axis_index("groups")
+    z = lax.axis_index("expert")
+    r = lax.axis_index("rep")
+    x = r // 2
+    c = lax.rem(r, 2)
+    p = x * G + g
+    mate = {"rep": x * 2 + 1 - c}
+    steps = [(i, j) for i in range(NX) for j in range(G) if i or j]
+    steps.sort(key=lambda s: -(min(s[0], NX - s[0]) + min(s[1], G - s[1])))
+
+    def plane_peer(step):
+        px, pg = lax.rem(x + step[0], NX), lax.rem(g + step[1], G)
+        return px * G + pg, {"groups": pg, "rep": px * 2 + c}
+
+    def signal(sem, device):
+        pl.semaphore_signal(sem, inc=1, device_id=device, device_id_type=MESH)
+
+    def remote(src, dst, send, recv, device):
+        return pltpu.make_async_remote_copy(
+            src_ref=src, dst_ref=dst, send_sem=send, recv_sem=recv, device_id=device, device_id_type=MESH
+        )
+
+    def landed(ref, sem):
+        pltpu.make_async_copy(ref, ref, sem).wait()
+
+    barrier = pltpu.get_barrier_semaphore()
+    for k in range(1, Z):
+        pl.when(z + k < Z)(lambda k=k: signal(barrier, {"expert": z + k}))
+    pl.when(z > 0)(lambda: signal(barrier, {"expert": z - 1}))
+    for step in steps:
+        signal(barrier, plane_peer(step)[1])
+    signal(barrier, mate)
+
+    def wide(q):
+        return pl.ds(pl.multiple_of(q * KC, KC), KC)
+
+    mine = pl.ds(pl.multiple_of(g * HH, HH), HH)
+    ids_copy = pltpu.make_async_copy(ids_hbm, ids_ref, small_sem.at[0])
+    probs_copy = pltpu.make_async_copy(probs_hbm, probs_ref, small_sem.at[1])
+    ids_copy.start()
+    probs_copy.start()
+
+    def own_copy(q):
+        return pltpu.make_async_copy(tok_hbm.at[:, wide(q)], blocks.at[q, c, p, z], tok_sem.at[q])
+
+    def gate_copy(q):
+        return pltpu.make_async_copy(gate_hbm.at[:, mine, wide(q)], pair_buf.at[q, :, 0], gate_sem.at[q])
+
+    def up_copy(q):
+        return pltpu.make_async_copy(up_hbm.at[:, mine, wide(q)], pair_buf.at[q, :, 1], up_sem.at[q])
+
+    def down_copy(k):
+        cols = pl.ds(pl.multiple_of(k * CW, CW), CW)
+        return pltpu.make_async_copy(down_hbm.at[:, mine, cols], down_buf.at[k], down_sem.at[k])
+
+    def load(q, carry):
+        own_copy(q).start()
+        return carry
+
+    lax.fori_loop(0, Q, load, 0)
+
+    def load_pair(q, carry):
+        gate_copy(q).start()
+        up_copy(q).start()
+        return carry
+
+    def load_down(k, carry):
+        down_copy(k).start()
+        return carry
+
+    lax.fori_loop(0, Q, load_pair, 0)
+    lax.fori_loop(0, CH, load_down, 0)
+
+    ids_copy.wait()
+    probs_copy.wait()
+    probs = probs_ref[...]
+    ids = ids_ref[...]
+    weights = probs / jnp.sum(probs, axis=1, keepdims=True)
+    lane = lax.broadcasted_iota(jnp.int32, (TOK, LANES), 1)
+    spot = lax.rem(lane, LANES // 2)
+    share = jnp.zeros((TOK, LANES), f32)
+    for k in range(ids.shape[1]):
+        share = share + jnp.where(ids[:, k : k + 1] == spot, weights[:, k : k + 1], 0.0)
+    high = share.astype(bf16).astype(f32)
+    route[c, p, z] = jnp.where(lane < LANES // 2, high, share - high).astype(bf16)
+
+    pl.semaphore_wait(barrier, z + 1 - (z + 1) // Z + P)
+
+    def block(q, where):
+        if q is None:
+            return route.at[where]
+        return blocks.at[(q, *where)]
+
+    def slot(q):
+        return Q if q is None else q
+
+    def z_copy(q, s, src, send, to):
+        return remote(src, block(q, (c, p, s)), send, z_recv.at[slot(q), s], {"expert": to})
+
+    def plane_copies(q, s, src):
+        for step in steps:
+            remote(
+                src, block(q, (c, p, s)), plane_send.at[slot(q)], plane_recv.at[slot(q)], plane_peer(step)[1]
+            ).start()
+
+    def spread(q):
+        src = route.at[c, p, z] if q is None else tok_hbm.at[:, wide(q)]
+        for k in range(Z - 1, 0, -1):
+            pl.when(z >= k)(lambda k=k: z_copy(q, z, src, fall_send.at[slot(q)], z - k).start())
+        pl.when(z < Z - 1)(lambda: z_copy(q, z, src, rise_send.at[slot(q)], z + 1).start())
+        plane_copies(q, z, src)
+
+    def pass_on(q):
+        for k in range(1, Z):
+
+            @pl.when(z >= k)
+            def _(k=k):
+                s = z - k
+                here = block(q, (c, p, s))
+                landed(here, z_recv.at[slot(q), s])
+                pl.when(z < Z - 1)(lambda: z_copy(q, s, here, rise_send.at[slot(q)], z + 1).start())
+                plane_copies(q, s, here)
+
+            @pl.when(z + k < Z)
+            def _(k=k):
+                s = z + k
+                here = block(q, (c, p, s))
+                landed(here, z_recv.at[slot(q), s])
+                plane_copies(q, s, here)
+
+    def to_mate(q):
+        landed(block(q, (0, pl.ds(0, P - 1))), plane_recv.at[slot(q)])
+        here = block(q, (c,))
+        remote(here, here, mate_send.at[slot(q)], mate_recv.at[slot(q)], mate).start()
+
+    def from_mate(q):
+        landed(block(q, (1 - c,)), mate_recv.at[slot(q)])
+
+    def loop(action, count):
+        def step(q, carry):
+            action(q)
+            return carry
+
+        lax.fori_loop(0, count, step, 0)
+
+    loop(spread, Q)
+    spread(None)
+    loop(lambda q: own_copy(q).wait(), Q)
+    loop(pass_on, Q)
+    pass_on(None)
+    acc_ref[...] = jnp.zeros_like(acc_ref)
+    to_mate(0)
+    nt = (((1,), (1,)), ((), ()))
+
+    def advance(q):
+        pl.when(q + 1 < Q)(lambda: to_mate(q + 1))
+        pl.when(q + 1 == Q)(lambda: to_mate(None))
+        from_mate(q)
+
+        def gather(i, carry):
+            at = pl.ds(pl.multiple_of(i * ZT, ZT), ZT)
+            rows_ref[at, :] = jnp.concatenate(
+                [blocks[q, i // P, lax.rem(i, P), k].astype(f32) for k in range(Z)], axis=0
+            ).astype(bf16)
+            return carry
+
+        lax.fori_loop(0, 2 * P, gather, 0)
+        gate_copy(q).wait()
+        up_copy(q).wait()
+        acc_ref[...] += lax.dot_general(
+            pair_buf[q].reshape(EL * 2 * HH, KC), rows_ref[...], nt, preferred_element_type=f32
+        )
+
+    loop(advance, Q)
+
+    from_mate(None)
+    table = jnp.concatenate(
+        [route[i // P, i % P, k].astype(f32) for i in range(2 * P) for k in range(Z)], axis=0
+    ).T
+    weight_ref[...] = table[: LANES // 2] + table[LANES // 2 :]
+
+    def activate(e):
+        gate = acc_ref[pl.ds(pl.multiple_of(e * 2 * HH, HH), HH), :]
+        up = acc_ref[pl.ds(pl.multiple_of(e * 2 * HH + HH, HH), HH), :]
+        scale = weight_ref[pl.ds(z * EL + e, 1), :]
+        at = pl.ds(pl.multiple_of(e * HH, HH), HH)
+        hid_ref[at, :] = gate / (1.0 + jnp.exp(-gate)) * up * scale
+
+    loop(activate, EL)
+    cat_ref[...] = hid_ref[...].T.astype(bf16)
+
+    def multiply(k):
+        down_copy(k).wait()
+        part_ref[...] = jnp.dot(
+            cat_ref[...], down_buf[k].reshape(EL * HH, CW), preferred_element_type=f32
+        ).reshape(2, HALF, CW)
+        own_a[k] = part_ref[c]
+        send_a[k] = part_ref[1 - c].astype(bf16)
+        remote(send_a.at[k], recv_a.at[k], a_send_sem.at[k], a_recv_sem.at[k], mate).start()
+
+    def first(k):
+        landed(recv_a.at[k], a_recv_sem.at[k])
+        total = own_a[k] + recv_a[k].astype(f32)
+        sum_ref[...] = total.reshape(P, ZT, CW)
+        own_b[k] = sum_ref[p]
+        send_b[k] = total.astype(bf16).reshape(P, ZT, CW)
+        for i, step in enumerate(steps):
+            there, device = plane_peer(step)
+            remote(send_b.at[k, there], recv_b.at[k, i], b_send_sem.at[k], b_recv_sem.at[k], device).start()
+
+    def second(k):
+        landed(recv_b.at[k], b_recv_sem.at[k])
+        total = own_b[k]
+        for i in range(P - 1):
+            total = total + recv_b[k, i].astype(f32)
+        for i in range(Z):
+            piece = total[i * TOK : (i + 1) * TOK, :]
+            own_c[k, i] = piece
+            send_c[k, i] = piece.astype(bf16)
+        for i in range(1, Z):
+            there = lax.rem(z + i, Z)
+            remote(
+                send_c.at[k, there], recv_c.at[k, i - 1], c_send_sem.at[k], c_recv_sem.at[k], {"expert": there}
+            ).start()
+
+    def third(k):
+        landed(recv_c.at[k], c_recv_sem.at[k])
+        total = own_c[k, z]
+        for i in range(1, Z):
+            total = total + recv_c[k, i - 1].astype(f32)
+        out_ref[:, pl.ds(pl.multiple_of(k * CW, CW), CW)] = total.astype(bf16)
+
+    def produce(k):
+        multiply(k)
+        pl.when(k >= FIRST_LAG)(lambda: first(k - FIRST_LAG))
+
+    loop(produce, CH)
+    lax.fori_loop(CH - FIRST_LAG, CH, lambda k, carry: (first(k), carry)[1], 0)
+    loop(second, CH)
+    loop(third, CH)
+
+    def settle(q):
+        for k in range(1, Z):
+            pl.when(z == k)(lambda k=k: landed(block(q, (0, 0, pl.ds(0, k))), fall_send.at[slot(q)]))
+        for k in range(Z - 1):
+            pl.when(z == k)(lambda k=k: landed(block(q, (0, 0, pl.ds(0, k + 1))), rise_send.at[slot(q)]))
+        landed(block(q, (0, pl.ds(0, P - 1))), plane_send.at[slot(q)])
+        landed(block(q, (0,)), mate_send.at[slot(q)])
+
+    loop(settle, Q)
+    settle(None)
+
+    def drain(k):
+        landed(recv_a.at[k], a_send_sem.at[k])
+        landed(recv_b.at[k], b_send_sem.at[k])
+        landed(recv_c.at[k], c_send_sem.at[k])
+
+    loop(drain, CH)
+
+
+def shared_call(mesh, args):
+    tokens, _, _, gate_weight, _, _ = args
+    G, Z, R = mesh.shape["groups"], mesh.shape["expert"], mesh.shape["rep"]
+    TOK, D = tokens.shape
+    EL, HID, _ = gate_weight.shape
+    if HID % (16 * G) or (Z * TOK) % 16 or Z * EL > LANES // 2 or D % (LANES * max(PIECES, CHUNKS)):
+        return None
+    HH, P, Q, CH = HID // G, R // 2 * G, PIECES, CHUNKS
+    KC, CW, ZT = D // Q, D // CH, Z * TOK
+    HALF = P * ZT
+    T = 2 * HALF
+    if (EL * HH) % LANES or T % LANES:
+        return None
+    bf16, f32 = jnp.bfloat16, jnp.float32
+    arrays = [
+        ((Q, 2, P, Z, TOK, KC), bf16),
+        ((2, P, Z, TOK, LANES), bf16),
+        ((TOK, LANES), jnp.int32),
+        ((TOK, LANES), f32),
+        ((T, KC), bf16),
+        ((LANES // 2, T), f32),
+        ((Q, EL, 2, HH, KC), bf16),
+        ((CH, EL, HH, CW), bf16),
+        ((EL * 2 * HH, T), f32),
+        ((EL * HH, T), f32),
+        ((T, EL * HH), bf16),
+        ((2, HALF, CW), f32),
+        ((CH, HALF, CW), f32),
+        ((CH, HALF, CW), bf16),
+        ((CH, HALF, CW), bf16),
+        ((P, ZT, CW), f32),
+        ((CH, ZT, CW), f32),
+        ((CH, P, ZT, CW), bf16),
+        ((CH, P - 1, ZT, CW), bf16),
+        ((CH, Z, TOK, CW), f32),
+        ((CH, Z, TOK, CW), bf16),
+        ((CH, Z - 1, TOK, CW), bf16),
+    ]
+    if sum(math.prod(shape) * jnp.dtype(dtype).itemsize for shape, dtype in arrays) > SHARED_BYTES:
+        return None
+    topk = args[1].shape[1]
+    arrays[2] = ((TOK, topk), jnp.int32)
+    arrays[3] = ((TOK, topk), f32)
+    vmem = pl.BlockSpec(memory_space=pltpu.VMEM)
+    hbm = pl.BlockSpec(memory_space=pl.ANY)
+    dma = pltpu.SemaphoreType.DMA
+    counts = [(Q,), (2,), (Q,), (Q,), (CH,), (Q + 1,), (Q + 1,), (Q + 1, Z)]
+    counts += [(Q + 1,)] * 4 + [(CH,)] * 6
+    return pl.pallas_call(
+        functools.partial(shared_kernel, (G, Z, R, EL, HH, TOK, D, Q, CH)),
+        out_shape=jax.ShapeDtypeStruct((TOK, D), bf16),
+        in_specs=[hbm] * 6,
+        out_specs=vmem,
+        scratch_shapes=[pltpu.VMEM(*a) for a in arrays] + [dma(n) for n in counts],
+        compiler_params=pltpu.CompilerParams(
+            collective_id=0, has_side_effects=True, vmem_limit_bytes=67_043_328
+        ),
+    )(*args)
+
+
 def solution(mesh):
     Z, R = mesh.shape["expert"], mesh.shape["rep"]
 
     def local(tokens, expert_ids, route_probs, gate_weight, up_weight, down_weight):
+        args = (tokens, expert_ids, route_probs, gate_weight, up_weight, down_weight)
+        shared = shared_call(mesh, args)
+        if shared is not None:
+            return shared
         TOK, D = tokens.shape
         EL, HID, _ = gate_weight.shape
         NB = min(DEPTH, EL)
@@ -295,7 +681,7 @@
         hbm = pl.BlockSpec(memory_space=pl.ANY)
         dma = pltpu.SemaphoreType.DMA
         return pl.pallas_call(
-            functools.partial(kernel, (Z, R, EL, TOK, D, CW, NB)),
+            functools.partial(wide_kernel, (Z, R, EL, TOK, D, CW, NB)),
             out_shape=jax.ShapeDtypeStruct((TOK, D), bf16),
             in_specs=[vmem, vmem, vmem, hbm, hbm, hbm],
             out_specs=vmem,

time: 44.5 us -> 42.3 us (0.951)
  Pallas kernels: 42.9 us -> 40.8 us
    pallas_call x1, Pallas kernels: 42.9 us -> 40.8 us  [shared_call(): pl.pallas_call(functools.partial(shared_kernel, (G, Z, R, EL, HH, TOK, D,...]
where the time goes in v1:
time: 42.3 us; the launch traced here: 42.1 us
  Pallas kernels  40.8 us (96%)
  local copies, waits for them, and re-layouts  1.39 us (3%)
    pallas_call x1, Pallas kernels, shared_call(): pl.pallas_call(functools.partial(shared_kernel, (G, Z, R, EL, HH, TOK, D,...  40.8 us
    unnamed x1, local copies, waits for them, and re-layouts  1.39 us

profile of v1, /device:TPU:0, one launch (start us, length us, event | category | flops | bytes accessed | tf_op | source)
XLA Modules:
  0.0 42.1 jit_solution(2992001596698464594)
XLA Ops:
  0.0 40.8 %shard_map.64 = bf16[4,4096]{1,0:T(4,128)(2,1)} custom-call(bf16[4,4096]{1,0:T(4,128)(2,1)} %tok_hbm.1, s32[4,8]{1,0:T(4,128)} %ids_hbm.1, f32[4,8]{1,0:T(4,128)} %probs_hbm.1, bf16[8,384,4096]{2,1,0:T(8,128)(2,1)} %gate_hbm.1, bf16[8,384,4096]{2,1,0:T(8,128)(2,1)} %up_hbm.1, bf16[8,384,4096]{2,1,0:T(8,128)(2,1)} %down_hbm.1), custom_call_target="tpu_custom_call" | custom-call | tf_op jit(solution)/shard_map/pallas_call | solution.py:653
  40.8 1.4 %copy.8 = bf16[4,4096]{1,0:T(4,128)(2,1)} copy(bf16[4,4096]{1,0:T(4,128)(2,1)} %shard_map.64) | data formatting | bytes 65536

commit v2 on v1

--- a/solution.py
+++ b/solution.py
@@ -14,7 +14,7 @@
 DEPTH = 5
 LAG = 5
 PIECES = 4
-FIRST_LAG = 3
+FIRST_LAG = 2
 SHARED_BYTES = 56 << 20
 
 
@@ -320,6 +320,8 @@
     gate_sem,
     up_sem,
     down_sem,
+    far_send,
+    far_recv,
     fall_send,
     rise_send,
     z_recv,
@@ -333,6 +335,7 @@
     b_recv_sem,
     c_send_sem,
     c_recv_sem,
+    ready,
 ):
     G, Z, R, EL, HH, TOK, D, Q, CH = dims
     NX = R // 2
@@ -415,6 +418,69 @@
     lax.fori_loop(0, Q, load_pair, 0)
     lax.fori_loop(0, CH, load_down, 0)
 
+    pl.semaphore_wait(barrier, z + 1 - (z + 1) // Z + P)
+
+    def block(q, where):
+        if q is None:
+            return route.at[where]
+        return blocks.at[(q, *where)]
+
+    def slot(q):
+        return Q if q is None else q
+
+    def z_copy(q, send, to):
+        src, dst = tok_hbm.at[:, wide(q)], blocks.at[q, c, p, z]
+        remote(src, dst, send.at[q], z_recv.at[q, z], {"expert": to}).start()
+
+    def plane_copies(q, s, src):
+        for step in steps:
+            remote(src, blocks.at[q, c, p, s], plane_send.at[q], plane_recv.at[q], plane_peer(step)[1]).start()
+
+    def spread(q):
+        for k in range(Z - 1, 0, -1):
+            pl.when(z >= k)(lambda k=k: z_copy(q, fall_send, z - k))
+        pl.when(z < Z - 1)(lambda: z_copy(q, rise_send, z + 1))
+        plane_copies(q, z, tok_hbm.at[:, wide(q)])
+
+    def spread_far(q):
+        for k in range(Z - 1, 1, -1):
+            pl.when(z + k < Z)(lambda k=k: z_copy(q, rise_send, z + k))
+
+    def arrive(q, s):
+        here = blocks.at[q, c, p, s]
+        landed(here, z_recv.at[q, s])
+        plane_copies(q, s, here)
+
+    def spread_route():
+        here = route.at[c, p, z]
+        for k in range(1, Z):
+            plane = lax.rem(z + k, Z)
+            remote(here, here, far_send, far_recv, {"expert": plane}).start()
+            for step in steps:
+                remote(here, here, plane_send.at[Q], plane_recv.at[Q], {"expert": plane, **plane_peer(step)[1]}).start()
+        for step in steps:
+            remote(here, here, plane_send.at[Q], plane_recv.at[Q], plane_peer(step)[1]).start()
+
+    def to_mate(q):
+        if q is None:
+            landed(route.at[0, 0, pl.ds(0, Z - 1)], far_recv)
+        landed(block(q, (0, pl.ds(0, P - 1))), plane_recv.at[slot(q)])
+        here = block(q, (c,))
+        remote(here, here, mate_send.at[slot(q)], mate_recv.at[slot(q)], mate).start()
+
+    def from_mate(q):
+        landed(block(q, (1 - c,)), mate_recv.at[slot(q)])
+
+    def loop(action, count):
+        def step(q, carry):
+            action(q)
+            return carry
+
+        lax.fori_loop(0, count, step, 0)
+
+    for k in range(2, Z):
+        pl.when(z >= k)(lambda k=k: signal(ready, {"expert": z - k}))
+    loop(spread, Q)
     ids_copy.wait()
     probs_copy.wait()
     probs = probs_ref[...]
@@ -428,72 +494,17 @@
     high = share.astype(bf16).astype(f32)
     route[c, p, z] = jnp.where(lane < LANES // 2, high, share - high).astype(bf16)
 
-    pl.semaphore_wait(barrier, z + 1 - (z + 1) // Z + P)
-
-    def block(q, where):
-        if q is None:
-            return route.at[where]
-        return blocks.at[(q, *where)]
-
-    def slot(q):
-        return Q if q is None else q
-
-    def z_copy(q, s, src, send, to):
-        return remote(src, block(q, (c, p, s)), send, z_recv.at[slot(q), s], {"expert": to})
-
-    def plane_copies(q, s, src):
-        for step in steps:
-            remote(
-                src, block(q, (c, p, s)), plane_send.at[slot(q)], plane_recv.at[slot(q)], plane_peer(step)[1]
-            ).start()
-
-    def spread(q):
-        src = route.at[c, p, z] if q is None else tok_hbm.at[:, wide(q)]
-        for k in range(Z - 1, 0, -1):
-            pl.when(z >= k)(lambda k=k: z_copy(q, z, src, fall_send.at[slot(q)], z - k).start())
-        pl.when(z < Z - 1)(lambda: z_copy(q, z, src, rise_send.at[slot(q)], z + 1).start())
-        plane_copies(q, z, src)
-
-    def pass_on(q):
-        for k in range(1, Z):
-
-            @pl.when(z >= k)
-            def _(k=k):
-                s = z - k
-                here = block(q, (c, p, s))
-                landed(here, z_recv.at[slot(q), s])
-                pl.when(z < Z - 1)(lambda: z_copy(q, s, here, rise_send.at[slot(q)], z + 1).start())
-                plane_copies(q, s, here)
-
-            @pl.when(z + k < Z)
-            def _(k=k):
-                s = z + k
-                here = block(q, (c, p, s))
-                landed(here, z_recv.at[slot(q), s])
-                plane_copies(q, s, here)
-
-    def to_mate(q):
-        landed(block(q, (0, pl.ds(0, P - 1))), plane_recv.at[slot(q)])
-        here = block(q, (c,))
-        remote(here, here, mate_send.at[slot(q)], mate_recv.at[slot(q)], mate).start()
-
-    def from_mate(q):
-        landed(block(q, (1 - c,)), mate_recv.at[slot(q)])
-
-    def loop(action, count):
-        def step(q, carry):
-            action(q)
-            return carry
-
-        lax.fori_loop(0, count, step, 0)
-
-    loop(spread, Q)
-    spread(None)
     loop(lambda q: own_copy(q).wait(), Q)
-    loop(pass_on, Q)
-    pass_on(None)
+    for k in range(1, Z):
+        pl.when(z >= k)(lambda k=k: loop(lambda q: arrive(q, z - k), Q))
+    for k in range(1, Z - 1):
+        pl.when(z == Z - 2 - k)(lambda k=k: pl.semaphore_wait(ready, k))
+    loop(spread_far, Q)
+    for k in range(1, Z):
+        pl.when(z + k < Z)(lambda k=k: loop(lambda q: arrive(q, z + k), Q))
     acc_ref[...] = jnp.zeros_like(acc_ref)
     to_mate(0)
+    spread_route()
     nt = (((1,), (1,)), ((), ()))
 
     def advance(q):
@@ -586,13 +597,15 @@
     def settle(q):
         for k in range(1, Z):
             pl.when(z == k)(lambda k=k: landed(block(q, (0, 0, pl.ds(0, k))), fall_send.at[slot(q)]))
-        for k in range(Z - 1):
-            pl.when(z == k)(lambda k=k: landed(block(q, (0, 0, pl.ds(0, k + 1))), rise_send.at[slot(q)]))
+        for k in range(1, Z):
+            pl.when(z == Z - 1 - k)(lambda k=k: landed(block(q, (0, 0, pl.ds(0, k))), rise_send.at[slot(q)]))
         landed(block(q, (0, pl.ds(0, P - 1))), plane_send.at[slot(q)])
         landed(block(q, (0,)), mate_send.at[slot(q)])
 
     loop(settle, Q)
-    settle(None)
+    landed(route.at[0, 0, pl.ds(0, Z - 1)], far_send)
+    landed(route.at[0, pl.ds(0, P - 1)], plane_send.at[Q])
+    landed(route.at[0], mate_send.at[Q])
 
     def drain(k):
         landed(recv_a.at[k], a_send_sem.at[k])
@@ -648,16 +661,16 @@
     vmem = pl.BlockSpec(memory_space=pltpu.VMEM)
     hbm = pl.BlockSpec(memory_space=pl.ANY)
     dma = pltpu.SemaphoreType.DMA
-    counts = [(Q,), (2,), (Q,), (Q,), (CH,), (Q + 1,), (Q + 1,), (Q + 1, Z)]
+    counts = [(Q,), (2,), (Q,), (Q,), (CH,), (), (), (Q,), (Q,), (Q, Z)]
     counts += [(Q + 1,)] * 4 + [(CH,)] * 6
     return pl.pallas_call(
         functools.partial(shared_kernel, (G, Z, R, EL, HH, TOK, D, Q, CH)),
-        out_shape=jax.ShapeDtypeStruct((TOK, D), bf16),
+        out_shape=pltpu.VMEM((TOK, D), bf16),
         in_specs=[hbm] * 6,
         out_specs=vmem,
-        scratch_shapes=[pltpu.VMEM(*a) for a in arrays] + [dma(n) for n in counts],
+        scratch_shapes=[pltpu.VMEM(*a) for a in arrays] + [dma(n) if n else dma for n in counts] + [pltpu.SemaphoreType.REGULAR],
         compiler_params=pltpu.CompilerParams(
-            collective_id=0, has_side_effects=True, vmem_limit_bytes=67_043_328
+            collective_id=0, has_side_effects=True, vmem_limit_bytes=SHARED_BYTES
         ),
     )(*args)
 

time: 42.3 us -> 38.9 us (0.920)
  Pallas kernels: 40.8 us -> 38.1 us
  local copies, waits for them, and re-layouts: 1.39 us -> 0.62 us
    pallas_call x1, Pallas kernels: 40.8 us -> 38.1 us  [shared_call(): pl.pallas_call(functools.partial(shared_kernel, (G, Z, R, EL, HH, TOK, D,...]
    unnamed x1, local copies, waits for them, and re-layouts: 1.39 us -> 0.62 us
where the time goes in v2:
time: 38.9 us; the launch traced here: 38.7 us
  Pallas kernels  38.1 us (98%)
  local copies, waits for them, and re-layouts  0.62 us (2%)
    pallas_call x1, Pallas kernels, shared_call(): pl.pallas_call(functools.partial(shared_kernel, (G, Z, R, EL, HH, TOK, D,...  38.1 us

profile of v2, /device:TPU:0, one launch (start us, length us, event | category | flops | bytes accessed | tf_op | source)
XLA Modules:
  0.0 38.7 jit_solution(18432220172706788364)
XLA Ops:
  0.0 38.1 %shard_map.64 = bf16[4,4096]{1,0:T(4,128)(2,1)S(1)} custom-call(bf16[4,4096]{1,0:T(4,128)(2,1)} %tok_hbm.1, s32[4,8]{1,0:T(4,128)} %ids_hbm.1, f32[4,8]{1,0:T(4,128)} %probs_hbm.1, bf16[8,384,4096]{2,1,0:T(8,128)(2,1)} %gate_hbm.1, bf16[8,384,4096]{2,1,0:T(8,128)(2,1)} %up_hbm.1, bf16[8,384,4096]{2,1,0:T(8,128)(2,1)} %down_hbm.1), custom_call_target="tpu_custom_call" | custom-call | tf_op jit(solution)/shard_map/pallas_call | solution.py:666
  38.1 0.6 %copy.8 = bf16[4,4096]{1,0:T(4,128)(2,1)} copy(bf16[4,4096]{1,0:T(4,128)(2,1)S(1)} %shard_map.64) | data formatting | bytes 65536
